TPU v7x, 32 devices: a whole 2x2x4 slice. The times are simulated.
32 devices in a mesh: groups: 2 (over y), ctx: 4 (over z), wt: 2 (over x), sub: 2 (over core).
Axes of the slice: x: 2, y: 2, z: 4, core: 2. Of those that a mesh axis runs over, the one named last changes fastest.
Arguments:
- queries: bfloat16 [16, 32, 128, 576], P(('groups', 'ctx'), None, ('wt', 'sub')), parts along dimension 0, may hold values from -80 to 80
- selection: int32 [16, 4, 2], P(('groups', 'ctx')), parts along dimension 0, may hold values from -1 to 15, as said below
- latent_cache: bfloat16 [128, 64, 576], P(('groups', 'ctx')), parts along dimension 0, may hold values from -8 to 8
- value_up: bfloat16 [128, 512, 128], P(None, ('wt', 'sub')), may hold values from -1 to 1
Outputs:
- attended: bfloat16 [16, 32, 128, 128], P(('groups', 'ctx'), None, ('wt', 'sub')), parts along dimension 0
There are 2 independent parts, one for each index of `groups`. A program takes and returns all parts, laid end to end along the dimension named above; an argument that names none is the same for every part. Nothing has to cross between parts.
Inputs may be any that keep to these rules, and one draw needn't show every extreme that they name: `selection`: entry [c, o, s] is the number of a block among the 16 of owner o, or -1 for an empty slot; in an owner's slots live entries come first and differ. Each query block has 4 live entries in all, and in every query block some owner fills all 2 slots.
All inputs are finite; a program needn't handle non-finite values.
Results may differ from a plain program's by a relative error of at most 0.008.
Values may be sent and summed in bfloat16 or wider, within the bound.
No kernel may reach another device: no remote copies, remote signals or barrier semaphores. Data moves between devices by JAX's collectives and lax.ppermute only.
A program may use at most 128 MiB of HBM per device.

v0:
```python
import jax
import jax.numpy as jnp
from jax import lax
from jax.sharding import PartitionSpec as P

LAT = 512
ROPE = 64
NOPE = 128


def attend(query, blocks, chosen):
    width = query.shape[2]
    owners = chosen.shape[0]
    count = chosen.shape[0] * chosen.shape[1]
    live = (chosen >= 0).reshape(-1)
    ranked = jnp.where(live, 0, count).astype(jnp.int32) + jnp.arange(count, dtype=jnp.int32)
    picked = jnp.argsort(ranked)[:owners]
    keys = blocks.reshape(count, blocks.shape[2], width)[picked].reshape(-1, width)
    rows = query.reshape(-1, width)
    scores = jnp.einsum("rd,kd->rk", rows, keys, preferred_element_type=jnp.float32)
    scores = scores * jnp.float32((NOPE + ROPE) ** (-0.5))
    expo = jnp.exp(scores - jnp.max(scores, axis=1, keepdims=True))
    totals = jnp.sum(expo, axis=1, keepdims=True)
    weights = expo.astype(jnp.bfloat16)
    latent = (jnp.dot(weights, keys[:, :LAT], preferred_element_type=jnp.float32) / totals).astype(
        jnp.bfloat16
    )
    return latent.reshape(query.shape[0], query.shape[1], LAT)


def per_device(queries, selection, latent_cache, value_up):
    owners = lax.axis_size("ctx")
    spans, per_span, heads_here, width = queries.shape
    slots = selection.shape[2]
    block_len = latent_cache.shape[1]

    def serve(asked):
        safe = jnp.clip(asked, 0, latent_cache.shape[0] - 1)
        return lax.all_to_all(latent_cache[safe], "ctx", split_axis=0, concat_axis=0, tiled=True)

    def fetch(wanted):
        half = slots // 2
        mine = lax.dynamic_slice_in_dim(wanted, lax.axis_index("sub") * half, half, 2)
        count = mine.shape[1] * mine.shape[2]
        fetched = serve(
            lax.all_to_all(
                mine.reshape(owners, count), "ctx", split_axis=0, concat_axis=0, tiled=True
            )
        )
        fetched = fetched.reshape(owners, mine.shape[1], mine.shape[2], block_len, width)
        fetched = lax.all_gather(fetched, "sub", axis=2, tiled=True)
        return fetched

    wanted_all = jnp.transpose(selection, (1, 0, 2))
    gathered = [fetch(wanted_all[:, index : index + 1])[:, 0] for index in range(spans)]
    latents = [attend(queries[index], gathered[index], selection[index]) for index in range(spans)]
    flat = jnp.stack(latents).reshape(spans * per_span, heads_here, LAT)
    my_weights = lax.all_to_all(value_up, ("wt", "sub"), split_axis=0, concat_axis=1, tiled=True)
    summed = jnp.einsum("nhl,hlv->nhv", flat, my_weights, preferred_element_type=jnp.float32)
    return summed.astype(jnp.bfloat16).reshape(spans, per_span, heads_here, my_weights.shape[2])


def solution(mesh):
    placed = (
        P(("groups", "ctx"), None, ("wt", "sub"), None),
        P(("groups", "ctx"), None, None),
        P(("groups", "ctx"), None, None),
        P(None, ("wt", "sub"), None),
    )
    return jax.shard_map(
        per_device,
        mesh=mesh,
        in_specs=placed,
        out_specs=P(("groups", "ctx"), None, ("wt", "sub"), None),
        check_vma=False,
    )
```

profile of v0, /device:TPU:0, one launch (start us, length us, event | category | flops | bytes accessed | tf_op | source)
XLA Modules:
  0.0 102.0 jit_solution(10457877809274622)
XLA Ops:
  0.0 0.9 copy.21
  1.6 6.3 %all-to-all-start = ((s32[4,1,1]{2,1,0:T(1,128)}), s32[4,1,1]{2,1,0:T(1,128)S(1)}, u32[]{:S(2)}, u32[]{:S(2)}) async-start(s32[4,1,1]{2,1,0:T(1,128)} %constant_dynamic-slice_fusion.1), calls=%async_computation | async-start | bytes 4096 | tf_op jit(solution)/shard_map/all_to_all | solution.py:46
  8.6 4.8 %all-to-all-done = s32[4,1,1]{2,1,0:T(1,128)S(1)} async-done(((s32[4,1,1]{2,1,0:T(1,128)}), s32[4,1,1]{2,1,0:T(1,128)S(1)}, u32[]{:S(2)}, u32[]{:S(2)}) %all-to-all-start) | async-done | bytes 48 | tf_op jit(solution)/shard_map/all_to_all | solution.py:46
  13.3 3.2 %all-to-all-start.2 = ((s32[4,1,1]{2,1,0:T(1,128)}), s32[4,1,1]{2,1,0:T(1,128)S(1)}, u32[]{:S(2)}, u32[]{:S(2)}) async-start(s32[4,1,1]{2,1,0:T(1,128)} %constant_dynamic-slice_fusion), calls=%async_computation.2 | async-start | bytes 4096 | tf_op jit(solution)/shard_map/all_to_all | solution.py:46
  16.7 1.3 %gather_fusion = bf16[4,64,576]{2,1,0:T(8,128)(2,1)} fusion(bf16[16,64,576]{2,1,0:T(8,128)(2,1)S(1)} %copy-done, s32[1024]{0:T(1024)S(1)} %pad_clamp_fusion.3), kind=kCustom, calls=%fused_computation | custom fusion | bytes 589840 | tf_op jit(solution)/shard_map/gather | solution.py:39
  18.0 4.0 %all-to-all-done.2 = s32[4,1,1]{2,1,0:T(1,128)S(1)} async-done(((s32[4,1,1]{2,1,0:T(1,128)}), s32[4,1,1]{2,1,0:T(1,128)S(1)}, u32[]{:S(2)}, u32[]{:S(2)}) %all-to-all-start.2) | async-done | bytes 48 | tf_op jit(solution)/shard_map/all_to_all | solution.py:46
  22.0 3.5 %all-to-all-start.1 = ((bf16[4,1,64,576]{3,2,1,0:T(8,128)(2,1)}), bf16[4,1,64,576]{3,2,1,0:T(8,128)(2,1)S(1)}, u32[]{:S(2)}, u32[]{:S(2)}) async-start(bf16[4,1,64,576]{3,2,1,0:T(8,128)(2,1)} %bitcast.1), calls=%async_computation.1 | async-start | bytes 655360 | tf_op jit(solution)/shard_map/all_to_all | solution.py:39
  25.7 1.3 %gather_fusion.2 = bf16[4,64,576]{2,1,0:T(8,128)(2,1)} fusion(bf16[16,64,576]{2,1,0:T(8,128)(2,1)S(1)} %copy-done, s32[1024]{0:T(1024)S(1)} %pad_clamp_fusion.1), kind=kCustom, calls=%fused_computation.2 | custom fusion | bytes 589840 | tf_op jit(solution)/shard_map/gather | solution.py:39
  27.0 5.8 %all-to-all-done.1 = bf16[4,1,64,576]{3,2,1,0:T(8,128)(2,1)S(1)} async-done(((bf16[4,1,64,576]{3,2,1,0:T(8,128)(2,1)}), bf16[4,1,64,576]{3,2,1,0:T(8,128)(2,1)S(1)}, u32[]{:S(2)}, u32[]{:S(2)}) %all-to-all-start.1) | async-done | bytes 294944 | tf_op jit(solution)/shard_map/all_to_all | solution.py:39
  32.8 3.6 %all-to-all-start.3 = ((bf16[4,1,64,576]{3,2,1,0:T(8,128)(2,1)}), bf16[4,1,64,576]{3,2,1,0:T(8,128)(2,1)S(1)}, u32[]{:S(2)}, u32[]{:S(2)}) async-start(bf16[4,1,64,576]{3,2,1,0:T(8,128)(2,1)} %bitcast.6), calls=%async_computation.3 | async-start | bytes 655360 | tf_op jit(solution)/shard_map/all_to_all | solution.py:39
  36.7 6.9 %all-to-all-done.3 = bf16[4,1,64,576]{3,2,1,0:T(8,128)(2,1)S(1)} async-done(((bf16[4,1,64,576]{3,2,1,0:T(8,128)(2,1)}), bf16[4,1,64,576]{3,2,1,0:T(8,128)(2,1)S(1)}, u32[]{:S(2)}, u32[]{:S(2)}) %all-to-all-start.3) | async-done | bytes 294944 | tf_op jit(solution)/shard_map/all_to_all | solution.py:39
  44.4 4.9 %all-to-all-start.4 = ((bf16[128,128,128]{2,1,0:T(8,128)(2,1)}), bf16[128,128,128]{2,1,0:T(8,128)(2,1)}, u32[]{:S(2)}, u32[]{:S(2)}) async-start(bf16[128,128,128]{2,1,0:T(8,128)(2,1)} %param.7), calls=%async_computation.4 | async-start | bytes 8388608 | tf_op jit(solution)/shard_map/all_to_all | solution.py:58
  49.3 1.0 sort.31
  50.2 1.0 sort.32
  51.3 3.1 %fusion.12 = (bf16[1,32,32,576]{3,2,1,0:T(8,128)(2,1)S(1)}, bf16[1,32,32,576]{3,2,1,0:T(8,128)(2,1)}) fusion(bf16[2,32,32,576]{3,2,1,0:T(8,128)(2,1)} %param.4), kind=kLoop, calls=%fused_computation.36 | loop fusion | bytes 4718592 | tf_op jit(solution)/shard_map/slice | solution.py:56
  54.4 2.3 %all-gather.1 = bf16[4,2,64,576]{3,2,1,0:T(8,128)(2,1)S(1)} all-gather(bf16[4,1,64,576]{3,2,1,0:T(8,128)(2,1)S(1)} %copy-done.3), channel_id=3, replica_groups=mesh['groups'=2,'ctx'=4,'wt'=2,'sub'=2] {'sub'}, dimensions={1}, use_global_device_ids=true | all-gather | bytes 884736 | tf_op jit(solution)/shard_map/all_gather | solution.py:51
  56.7 1.3 %gather_fusion.3 = bf16[4,64,576]{2,1,0:T(8,128)(2,1)} fusion(bf16[8,64,576]{2,1,0:T(8,128)(2,1)S(1)} %bitcast.30, s32[1024]{0:T(1024)S(1)} %pad_clamp_fusion), kind=kCustom, calls=%fused_computation.3 | custom fusion | bytes 589840 | tf_op jit(solution)/shard_map/gather | solution.py:18
  58.0 2.5 %all-gather = bf16[4,2,64,576]{3,2,1,0:T(8,128)(2,1)S(1)} all-gather(bf16[4,1,64,576]{3,2,1,0:T(8,128)(2,1)} %copy-done.1), channel_id=2, replica_groups=mesh['groups'=2,'ctx'=4,'wt'=2,'sub'=2] {'sub'}, dimensions={1}, use_global_device_ids=true | all-gather | bytes 884736 | tf_op jit(solution)/shard_map/all_gather | solution.py:51
  60.5 1.3 %gather_fusion.1 = bf16[4,64,576]{2,1,0:T(8,128)(2,1)} fusion(bf16[8,64,576]{2,1,0:T(8,128)(2,1)S(1)} %bitcast.31, s32[1024]{0:T(1024)S(1)} %pad_clamp_fusion.2), kind=kCustom, calls=%fused_computation.1 | custom fusion | bytes 589840 | tf_op jit(solution)/shard_map/gather | solution.py:18
  61.8 2.1 %fusion.14 = (f32[1024]{0:T(1024)S(1)}, f32[256,1024]{1,0:T(8,128)S(1)}) fusion(bf16[256,576]{1,0:T(8,128)(2,1)} %bitcast.32, bf16[1024,576]{1,0:T(8,128)(2,1)} %bitcast.28), kind=kOutput, calls=%fused_computation.38 | convolution fusion | flops 302513152 | bytes 2527232 | tf_op jit(solution)/shard_map/rd,kd->rk/dot_general | solution.py:20
  66.3 1.2 %copy.24 = bf16[2,32,32,512]{3,1,0,2:T(8,128)(2,1)S(1)} copy(bf16[2,32,32,512]{3,2,1,0:T(8,128)(2,1)S(1)} %pad_maximum_fusion) | data formatting | bytes 4194304 | tf_op jit(solution)/shard_map/stack | solution.py:57
  67.4 30.0 %all-to-all-done.4 = bf16[128,128,128]{2,1,0:T(8,128)(2,1)} async-done(((bf16[128,128,128]{2,1,0:T(8,128)(2,1)}), bf16[128,128,128]{2,1,0:T(8,128)(2,1)}, u32[]{:S(2)}, u32[]{:S(2)}) %all-to-all-start.4) | async-done | bytes 4194336 | tf_op jit(solution)/shard_map/all_to_all | solution.py:58
  97.5 2.5 %copy.25 = bf16[4,32,128,128]{3,2,0,1:T(8,128)(2,1)S(1)} copy(bf16[4,32,128,128]{3,2,1,0:T(8,128)(2,1)} %bitcast.12) | data formatting | bytes 8388608 | tf_op jit(solution)/shard_map/all_to_all | solution.py:58
  100.8 1.1 %copy.26 = bf16[2,32,32,128]{3,2,1,0:T(8,128)(2,1)} copy(bf16[2,32,32,128]{3,1,0,2:T(8,128)(2,1)S(1)} %bitcast.29) | data formatting | bytes 1048576 | tf_op jit(solution)/shard_map/reshape | solution.py:60
  (41 shorter events, 6.0 us)
Async XLA Ops:
  0.0 16.7 %copy-start = (bf16[16,64,576]{2,1,0:T(8,128)(2,1)S(1)}, bf16[16,64,576]{2,1,0:T(8,128)(2,1)}, u32[]{:S(2)}) copy-start(bf16[16,64,576]{2,1,0:T(8,128)(2,1)} %param.6) | copy-start | bytes 3538948
  0.0 36.4 %copy-start.6 = (s32[2,4,2]{1,2,0:T(2,128)S(1)}, s32[2,4,2]{1,2,0:T(2,128)}, u32[]{:S(2)}) copy-start(s32[2,4,2]{1,2,0:T(2,128)} %param.5) | copy-start | bytes 196
  1.6 11.8 %all-to-all-start = ((s32[4,1,1]{2,1,0:T(1,128)}), s32[4,1,1]{2,1,0:T(1,128)S(1)}, u32[]{:S(2)}, u32[]{:S(2)}) async-start(s32[4,1,1]{2,1,0:T(1,128)} %constant_dynamic-slice_fusion.1), calls=%async_computation | async-start | bytes 4096 | tf_op jit(solution)/shard_map/all_to_all | solution.py:46
  13.3 8.7 %all-to-all-start.2 = ((s32[4,1,1]{2,1,0:T(1,128)}), s32[4,1,1]{2,1,0:T(1,128)S(1)}, u32[]{:S(2)}, u32[]{:S(2)}) async-start(s32[4,1,1]{2,1,0:T(1,128)} %constant_dynamic-slice_fusion), calls=%async_computation.2 | async-start | bytes 4096 | tf_op jit(solution)/shard_map/all_to_all | solution.py:46
  22.0 10.7 %all-to-all-start.1 = ((bf16[4,1,64,576]{3,2,1,0:T(8,128)(2,1)}), bf16[4,1,64,576]{3,2,1,0:T(8,128)(2,1)S(1)}, u32[]{:S(2)}, u32[]{:S(2)}) async-start(bf16[4,1,64,576]{3,2,1,0:T(8,128)(2,1)} %bitcast.1), calls=%async_computation.1 | async-start | bytes 655360 | tf_op jit(solution)/shard_map/all_to_all | solution.py:39
  32.8 10.9 %copy-start.1 = (bf16[4,1,64,576]{3,2,1,0:T(8,128)(2,1)}, bf16[4,1,64,576]{3,2,1,0:T(8,128)(2,1)S(1)}, u32[]{:S(2)}) copy-start(bf16[4,1,64,576]{3,2,1,0:T(8,128)(2,1)S(1)} %all-to-all-done.1) | copy-start | bytes 884740
  32.8 10.9 %all-to-all-start.3 = ((bf16[4,1,64,576]{3,2,1,0:T(8,128)(2,1)}), bf16[4,1,64,576]{3,2,1,0:T(8,128)(2,1)S(1)}, u32[]{:S(2)}, u32[]{:S(2)}) async-start(bf16[4,1,64,576]{3,2,1,0:T(8,128)(2,1)} %bitcast.6), calls=%async_computation.3 | async-start | bytes 655360 | tf_op jit(solution)/shard_map/all_to_all | solution.py:39
  43.7 0.7 copy-start.2
  44.4 53.1 %all-to-all-start.4 = ((bf16[128,128,128]{2,1,0:T(8,128)(2,1)}), bf16[128,128,128]{2,1,0:T(8,128)(2,1)}, u32[]{:S(2)}, u32[]{:S(2)}) async-start(bf16[128,128,128]{2,1,0:T(8,128)(2,1)} %param.7), calls=%async_computation.4 | async-start | bytes 8388608 | tf_op jit(solution)/shard_map/all_to_all | solution.py:58
  51.3 3.1 %copy-start.3 = (bf16[4,1,64,576]{3,2,1,0:T(8,128)(2,1)S(1)}, bf16[4,1,64,576]{3,2,1,0:T(8,128)(2,1)}, u32[]{:S(2)}) copy-start(bf16[4,1,64,576]{3,2,1,0:T(8,128)(2,1)} %copy-done.2) | copy-start | bytes 884740
  61.8 2.3 %copy-start.5 = (bf16[4,64,576]{2,1,0:T(8,128)(2,1)S(1)}, bf16[4,64,576]{2,1,0:T(8,128)(2,1)}, u32[]{:S(2)}) copy-start(bf16[4,64,576]{2,1,0:T(8,128)(2,1)} %gather_fusion.1) | copy-start | bytes 884740
  64.1 1.0 copy-start.4
where the time goes:
time: 103 us; the launch traced here: 102 us
  waiting for transfers between devices  51.5 us (50%)
  starting transfers between devices  21.5 us (21%)
  local copies, waits for them, and re-layouts  16.6 us (16%)
  blocking collectives  4.81 us (5%)
  matrix products  4.57 us (4%)
  other arithmetic  2.85 us (3%)
    all_to_all x1, waiting for transfers between devices, per_device(): lax.all_to_all(value_up, ('wt', 'sub'), split_axis=0, concat_axis=1, tile...  30 us
    all_to_all x2, waiting for transfers between devices, serve(): lax.all_to_all(latent_cache[safe], 'ctx', split_axis=0, concat_axis=0, ti...  12.7 us
    all_to_all x2, starting transfers between devices, fetch(): lax.all_to_all(mine.reshape(owners, count), 'ctx', split_axis=0, concat_a...  9.57 us
    all_to_all x2, waiting for transfers between devices, fetch(): lax.all_to_all(mine.reshape(owners, count), 'ctx', split_axis=0, concat_a...  8.76 us
    all_to_all x2, starting transfers between devices, serve(): lax.all_to_all(latent_cache[safe], 'ctx', split_axis=0, concat_axis=0, ti...  7.06 us
    all_to_all x1, starting transfers between devices, per_device(): lax.all_to_all(value_up, ('wt', 'sub'), split_axis=0, concat_axis=1, tile...  4.86 us
    all_gather x2, blocking collectives, fetch(): fetched = lax.all_gather(fetched, 'sub', axis=2, tiled=True)  4.81 us
    slice x1, local copies, waits for them, and re-layouts, per_device(): queries[index]  3.08 us
  transfers between devices with their start and end apart: 5, of which 5 were waited for; matrix products, arithmetic and copies ran while one was open for 17% of the time, Pallas kernels for 0%

commit v1 on v0

--- a/solution.py
+++ b/solution.py
@@ -6,6 +6,22 @@
 LAT = 512
 ROPE = 64
 NOPE = 128
+
+
+def pairwise_exchange(shard, axis, split, join):
+    ways, here = (lax.axis_size(axis), lax.axis_index(axis))
+    width = shard.shape[split] // ways
+    shape = list(shard.shape)
+    shape[split] = width
+    height = shape[join]
+    shape[join] = height * ways
+    full = jnp.zeros(shape, shard.dtype)
+    for mask in range(ways):
+        part = lax.dynamic_slice_in_dim(shard, (here ^ mask) * width, width, axis=split)
+        if mask:
+            part = lax.ppermute(part, axis, [(d, d ^ mask) for d in range(ways)])
+        full = lax.dynamic_update_slice_in_dim(full, part, (here ^ mask) * height, axis=join)
+    return full
 
 
 def attend(query, blocks, chosen):
@@ -42,11 +58,7 @@
         half = slots // 2
         mine = lax.dynamic_slice_in_dim(wanted, lax.axis_index("sub") * half, half, 2)
         count = mine.shape[1] * mine.shape[2]
-        fetched = serve(
-            lax.all_to_all(
-                mine.reshape(owners, count), "ctx", split_axis=0, concat_axis=0, tiled=True
-            )
-        )
+        fetched = serve(pairwise_exchange(mine.reshape(owners, count), "ctx", 0, 0))
         fetched = fetched.reshape(owners, mine.shape[1], mine.shape[2], block_len, width)
         fetched = lax.all_gather(fetched, "sub", axis=2, tiled=True)
         return fetched

time: 103 us -> 103 us (level)
  waiting for transfers between devices: 51.5 us -> 45 us
  local copies, waits for them, and re-layouts: 16.6 us -> 22.2 us
  starting transfers between devices: 21.5 us -> 22.8 us
    ppermute x0 -> x6, starting transfers between devices: none -> 10.2 us  [pairwise_exchange(): part = lax.ppermute(part, axis, [(d, d ^ mask) for d in range(ways)])]
    all_to_all x2 -> x0, starting transfers between devices: 9.57 us -> none  [fetch(): lax.all_to_all(mine.reshape(owners, count), 'ctx', split_axis=0, concat_a...]
    all_to_all x2 -> x0, waiting for transfers between devices: 8.76 us -> none  [fetch(): lax.all_to_all(mine.reshape(owners, count), 'ctx', split_axis=0, concat_a...]
    dynamic_update_slice x0 -> x8, local copies, waits for them, and re-layouts: none -> 5.69 us  [pairwise_exchange(): lax.dynamic_update_slice_in_dim(full, part, (here ^ mask) * height, axis=...]
    all_to_all x2, waiting for transfers between devices: 12.7 us -> 14 us  [serve(): lax.all_to_all(latent_cache[safe], 'ctx', split_axis=0, concat_axis=0, ti...]
  transfers between devices with their start and end apart: 5 -> 9, of which waited for: 5 -> 4; matrix products, arithmetic and copies ran while one was open for 17% -> 20% of each run, Pallas kernels for 0% -> 0%
where the time goes in v1:
time: 103 us; the launch traced here: 102 us
  waiting for transfers between devices  45 us (44%)
  starting transfers between devices  22.8 us (22%)
  local copies, waits for them, and re-layouts  22.2 us (22%)
  blocking collectives  4.81 us (5%)
  matrix products  4.56 us (4%)
  other arithmetic  2.53 us (2%)
    all_to_all x1, waiting for transfers between devices, per_device(): lax.all_to_all(value_up, ('wt', 'sub'), split_axis=0, concat_axis=1, tile...  30 us
    all_to_all x2, waiting for transfers between devices, serve(): lax.all_to_all(latent_cache[safe], 'ctx', split_axis=0, concat_axis=0, ti...  14 us
    ppermute x6, starting transfers between devices, pairwise_exchange(): part = lax.ppermute(part, axis, [(d, d ^ mask) for d in range(ways)])  10.2 us
    all_to_all x2, starting transfers between devices, serve(): lax.all_to_all(latent_cache[safe], 'ctx', split_axis=0, concat_axis=0, ti...  7.69 us
    dynamic_update_slice x8, local copies, waits for them, and re-layouts, pairwise_exchange(): lax.dynamic_update_slice_in_dim(full, part, (here ^ mask) * height, axis=...  5.69 us
    all_to_all x1, starting transfers between devices, per_device(): lax.all_to_all(value_up, ('wt', 'sub'), split_axis=0, concat_axis=1, tile...  4.86 us
    all_gather x2, blocking collectives, fetch(): fetched = lax.all_gather(fetched, 'sub', axis=2, tiled=True)  4.81 us
    slice x1, local copies, waits for them, and re-layouts, per_device(): queries[index]  3.08 us
  transfers between devices with their start and end apart: 9, of which 4 were waited for; matrix products, arithmetic and copies ran while one was open for 20% of the time, Pallas kernels for 0%

profile of v1, /device:TPU:0, one launch (start us, length us, event | category | flops | bytes accessed | tf_op | source)
XLA Modules:
  0.0 102.1 jit_solution(18001123323923653473)
XLA Ops:
  0.0 0.8 fusion.13
  1.5 5.1 %collective-permute-start.5 = (s32[1,1]{0,1:T(1,128)}, s32[1,1]{0,1:T(1,128)}, u32[]{:S(2)}, u32[]{:S(2)}) collective-permute-start(s32[1,1]{0,1:T(1,128)} %bitcast.14), channel_id=1, source_target_pairs={{0,12},{4,8},{8,4},{12,0},{1,13},{5,9},{9,5},{13,1},{2,14},{6,10},... | collective-permute-start | bytes 20 | tf_op jit(solution)/shard_map/ppermute | solution.py:22
  7.8 3.8 %collective-permute-start.2 = (s32[1,1]{0,1:T(1,128)}, s32[1,1]{0,1:T(1,128)}, u32[]{:S(2)}, u32[]{:S(2)}) collective-permute-start(s32[1,1]{0,1:T(1,128)} %bitcast.4), channel_id=1, source_target_pairs={{0,12},{4,8},{8,4},{12,0},{1,13},{5,9},{9,5},{13,1},{2,14},{6,10},... | collective-permute-start | bytes 20 | tf_op jit(solution)/shard_map/ppermute | solution.py:22
  15.8 1.0 collective-permute-done
  19.1 1.3 %gather_fusion.2 = bf16[4,64,576]{2,1,0:T(8,128)(2,1)} fusion(bf16[16,64,576]{2,1,0:T(8,128)(2,1)S(1)} %copy-done, s32[1024]{0:T(1024)S(1)} %pad_clamp_fusion.1), kind=kCustom, calls=%fused_computation.2 | custom fusion | bytes 589840 | tf_op jit(solution)/shard_map/gather | solution.py:55
  20.4 4.2 %all-to-all-start.1 = ((bf16[4,1,64,576]{3,2,1,0:T(8,128)(2,1)}), bf16[4,1,64,576]{3,2,1,0:T(8,128)(2,1)S(1)}, u32[]{:S(2)}, u32[]{:S(2)}) async-start(bf16[4,1,64,576]{3,2,1,0:T(8,128)(2,1)} %bitcast.16), calls=%async_computation.1 | async-start | bytes 655360 | tf_op jit(solution)/shard_map/all_to_all | solution.py:55
  24.6 1.3 %gather_fusion = bf16[4,64,576]{2,1,0:T(8,128)(2,1)} fusion(bf16[16,64,576]{2,1,0:T(8,128)(2,1)S(1)} %copy-done, s32[1024]{0:T(1024)S(1)} %pad_clamp_fusion.3), kind=kCustom, calls=%fused_computation | custom fusion | bytes 589840 | tf_op jit(solution)/shard_map/gather | solution.py:55
  25.9 7.1 %all-to-all-done.1 = bf16[4,1,64,576]{3,2,1,0:T(8,128)(2,1)S(1)} async-done(((bf16[4,1,64,576]{3,2,1,0:T(8,128)(2,1)}), bf16[4,1,64,576]{3,2,1,0:T(8,128)(2,1)S(1)}, u32[]{:S(2)}, u32[]{:S(2)}) %all-to-all-start.1) | async-done | bytes 294944 | tf_op jit(solution)/shard_map/all_to_all | solution.py:55
  33.0 3.5 %all-to-all-start = ((bf16[4,1,64,576]{3,2,1,0:T(8,128)(2,1)}), bf16[4,1,64,576]{3,2,1,0:T(8,128)(2,1)S(1)}, u32[]{:S(2)}, u32[]{:S(2)}) async-start(bf16[4,1,64,576]{3,2,1,0:T(8,128)(2,1)} %bitcast.6), calls=%async_computation | async-start | bytes 655360 | tf_op jit(solution)/shard_map/all_to_all | solution.py:55
  36.9 6.9 %all-to-all-done = bf16[4,1,64,576]{3,2,1,0:T(8,128)(2,1)S(1)} async-done(((bf16[4,1,64,576]{3,2,1,0:T(8,128)(2,1)}), bf16[4,1,64,576]{3,2,1,0:T(8,128)(2,1)S(1)}, u32[]{:S(2)}, u32[]{:S(2)}) %all-to-all-start) | async-done | bytes 294944 | tf_op jit(solution)/shard_map/all_to_all | solution.py:55
  44.5 4.9 %all-to-all-start.2 = ((bf16[128,128,128]{2,1,0:T(8,128)(2,1)}), bf16[128,128,128]{2,1,0:T(8,128)(2,1)}, u32[]{:S(2)}, u32[]{:S(2)}) async-start(bf16[128,128,128]{2,1,0:T(8,128)(2,1)} %param.7), calls=%async_computation.2 | async-start | bytes 8388608 | tf_op jit(solution)/shard_map/all_to_all | solution.py:70
  49.4 1.0 sort.31
  50.4 1.0 sort.32
  51.4 3.1 %fusion.12 = (bf16[1,32,32,576]{3,2,1,0:T(8,128)(2,1)S(1)}, bf16[1,32,32,576]{3,2,1,0:T(8,128)(2,1)}) fusion(bf16[2,32,32,576]{3,2,1,0:T(8,128)(2,1)} %param.4), kind=kLoop, calls=%fused_computation.42 | loop fusion | bytes 4718592 | tf_op jit(solution)/shard_map/slice | solution.py:68
  54.5 2.3 %all-gather = bf16[4,2,64,576]{3,2,1,0:T(8,128)(2,1)S(1)} all-gather(bf16[4,1,64,576]{3,2,1,0:T(8,128)(2,1)S(1)} %copy-done.3), channel_id=2, replica_groups=mesh['groups'=2,'ctx'=4,'wt'=2,'sub'=2] {'sub'}, dimensions={1}, use_global_device_ids=true | all-gather | bytes 884736 | tf_op jit(solution)/shard_map/all_gather | solution.py:63
  56.8 1.3 %gather_fusion.1 = bf16[4,64,576]{2,1,0:T(8,128)(2,1)} fusion(bf16[8,64,576]{2,1,0:T(8,128)(2,1)S(1)} %bitcast.42, s32[1024]{0:T(1024)S(1)} %pad_clamp_fusion.2), kind=kCustom, calls=%fused_computation.1 | custom fusion | bytes 589840 | tf_op jit(solution)/shard_map/gather | solution.py:34
  58.1 2.5 %all-gather.1 = bf16[4,2,64,576]{3,2,1,0:T(8,128)(2,1)S(1)} all-gather(bf16[4,1,64,576]{3,2,1,0:T(8,128)(2,1)} %copy-done.1), channel_id=3, replica_groups=mesh['groups'=2,'ctx'=4,'wt'=2,'sub'=2] {'sub'}, dimensions={1}, use_global_device_ids=true | all-gather | bytes 884736 | tf_op jit(solution)/shard_map/all_gather | solution.py:63
  60.6 1.3 %gather_fusion.3 = bf16[4,64,576]{2,1,0:T(8,128)(2,1)} fusion(bf16[8,64,576]{2,1,0:T(8,128)(2,1)S(1)} %bitcast.43, s32[1024]{0:T(1024)S(1)} %pad_clamp_fusion), kind=kCustom, calls=%fused_computation.3 | custom fusion | bytes 589840 | tf_op jit(solution)/shard_map/gather | solution.py:34
  61.9 2.1 %fusion.14 = (f32[1024]{0:T(1024)S(1)}, f32[256,1024]{1,0:T(8,128)S(1)}) fusion(bf16[256,576]{1,0:T(8,128)(2,1)} %bitcast.46, bf16[1024,576]{1,0:T(8,128)(2,1)} %bitcast.40), kind=kOutput, calls=%fused_computation.44 | convolution fusion | flops 302513152 | bytes 2527232 | tf_op jit(solution)/shard_map/rd,kd->rk/dot_general | solution.py:36
  66.3 1.2 %copy.12 = bf16[2,32,32,512]{3,1,0,2:T(8,128)(2,1)S(1)} copy(bf16[2,32,32,512]{3,2,1,0:T(8,128)(2,1)S(1)} %pad_maximum_fusion) | data formatting | bytes 4194304 | tf_op jit(solution)/shard_map/stack | solution.py:69
  67.5 30.0 %all-to-all-done.2 = bf16[128,128,128]{2,1,0:T(8,128)(2,1)} async-done(((bf16[128,128,128]{2,1,0:T(8,128)(2,1)}), bf16[128,128,128]{2,1,0:T(8,128)(2,1)}, u32[]{:S(2)}, u32[]{:S(2)}) %all-to-all-start.2) | async-done | bytes 4194336 | tf_op jit(solution)/shard_map/all_to_all | solution.py:70
  97.6 2.5 %copy.13 = bf16[4,32,128,128]{3,2,0,1:T(8,128)(2,1)S(1)} copy(bf16[4,32,128,128]{3,2,1,0:T(8,128)(2,1)} %bitcast.22) | data formatting | bytes 8388608 | tf_op jit(solution)/shard_map/all_to_all | solution.py:70
  100.1 0.9 convolution_convert_fusion
  100.9 1.1 %copy.14 = bf16[2,32,32,128]{3,2,1,0:T(8,128)(2,1)} copy(bf16[2,32,32,128]{3,1,0,2:T(8,128)(2,1)S(1)} %bitcast.41) | data formatting | bytes 1048576 | tf_op jit(solution)/shard_map/reshape | solution.py:72
  (57 shorter events, 11.8 us)
Async XLA Ops:
  0.0 19.1 %copy-start = (bf16[16,64,576]{2,1,0:T(8,128)(2,1)S(1)}, bf16[16,64,576]{2,1,0:T(8,128)(2,1)}, u32[]{:S(2)}) copy-start(bf16[16,64,576]{2,1,0:T(8,128)(2,1)} %param.6) | copy-start | bytes 3538948
  0.0 36.5 %copy-start.6 = (s32[2,4,2]{1,2,0:T(2,128)S(1)}, s32[2,4,2]{1,2,0:T(2,128)}, u32[]{:S(2)}) copy-start(s32[2,4,2]{1,2,0:T(2,128)} %param.5) | copy-start | bytes 196
  1.5 13.7 %collective-permute-start.5 = (s32[1,1]{0,1:T(1,128)}, s32[1,1]{0,1:T(1,128)}, u32[]{:S(2)}, u32[]{:S(2)}) collective-permute-start(s32[1,1]{0,1:T(1,128)} %bitcast.14), channel_id=1, source_target_pairs={{0,12},{4,8},{8,4},{12,0},{1,13},{5,9},{9,5},{13,1},{2,14},{6,10},... | collective-permute-start | bytes 20 | tf_op jit(solution)/shard_map/ppermute | solution.py:22
  6.6 7.9 %collective-permute-start.4 = (s32[1,1]{0,1:T(1,128)}, s32[1,1]{0,1:T(1,128)}, u32[]{:S(2)}, u32[]{:S(2)}) collective-permute-start(s32[1,1]{0,1:T(1,128)} %bitcast.13), channel_id=1, source_target_pairs={{0,8},{4,12},{8,0},{12,4},{1,9},{5,13},{9,1},{13,5},{2,10},{6,14},... | collective-permute-start | bytes 20 | tf_op jit(solution)/shard_map/ppermute | solution.py:22
  6.6 6.4 %collective-permute-start.3 = (s32[1,1]{0,1:T(1,128)}, s32[1,1]{0,1:T(1,128)}, u32[]{:S(2)}, u32[]{:S(2)}) collective-permute-start(s32[1,1]{0,1:T(1,128)} %bitcast.12), channel_id=1, source_target_pairs={{0,4},{4,0},{8,12},{12,8},{1,5},{5,1},{9,13},{13,9},{2,6},{6,2},{1... | collective-permute-start | bytes 20 | tf_op jit(solution)/shard_map/ppermute | solution.py:22
  7.8 10.5 %collective-permute-start.2 = (s32[1,1]{0,1:T(1,128)}, s32[1,1]{0,1:T(1,128)}, u32[]{:S(2)}, u32[]{:S(2)}) collective-permute-start(s32[1,1]{0,1:T(1,128)} %bitcast.4), channel_id=1, source_target_pairs={{0,12},{4,8},{8,4},{12,0},{1,13},{5,9},{9,5},{13,1},{2,14},{6,10},... | collective-permute-start | bytes 20 | tf_op jit(solution)/shard_map/ppermute | solution.py:22
  11.6 6.0 %collective-permute-start.1 = (s32[1,1]{0,1:T(1,128)}, s32[1,1]{0,1:T(1,128)}, u32[]{:S(2)}, u32[]{:S(2)}) collective-permute-start(s32[1,1]{0,1:T(1,128)} %bitcast.3), channel_id=1, source_target_pairs={{0,8},{4,12},{8,0},{12,4},{1,9},{5,13},{9,1},{13,5},{2,10},{6,14},... | collective-permute-start | bytes 20 | tf_op jit(solution)/shard_map/ppermute | solution.py:22
  13.0 3.8 %collective-permute-start = (s32[1,1]{0,1:T(1,128)}, s32[1,1]{0,1:T(1,128)}, u32[]{:S(2)}, u32[]{:S(2)}) collective-permute-start(s32[1,1]{0,1:T(1,128)} %bitcast.2), channel_id=1, source_target_pairs={{0,4},{4,0},{8,12},{12,8},{1,5},{5,1},{9,13},{13,9},{2,6},{6,2},{1... | collective-permute-start | bytes 20 | tf_op jit(solution)/shard_map/ppermute | solution.py:22
  20.4 12.6 %all-to-all-start.1 = ((bf16[4,1,64,576]{3,2,1,0:T(8,128)(2,1)}), bf16[4,1,64,576]{3,2,1,0:T(8,128)(2,1)S(1)}, u32[]{:S(2)}, u32[]{:S(2)}) async-start(bf16[4,1,64,576]{3,2,1,0:T(8,128)(2,1)} %bitcast.16), calls=%async_computation.1 | async-start | bytes 655360 | tf_op jit(solution)/shard_map/all_to_all | solution.py:55
  33.0 10.7 %copy-start.1 = (bf16[4,1,64,576]{3,2,1,0:T(8,128)(2,1)}, bf16[4,1,64,576]{3,2,1,0:T(8,128)(2,1)S(1)}, u32[]{:S(2)}) copy-start(bf16[4,1,64,576]{3,2,1,0:T(8,128)(2,1)S(1)} %all-to-all-done.1) | copy-start | bytes 884740
  33.0 10.7 %all-to-all-start = ((bf16[4,1,64,576]{3,2,1,0:T(8,128)(2,1)}), bf16[4,1,64,576]{3,2,1,0:T(8,128)(2,1)S(1)}, u32[]{:S(2)}, u32[]{:S(2)}) async-start(bf16[4,1,64,576]{3,2,1,0:T(8,128)(2,1)} %bitcast.6), calls=%async_computation | async-start | bytes 655360 | tf_op jit(solution)/shard_map/all_to_all | solution.py:55
  43.7 0.8 copy-start.2
  44.5 53.1 %all-to-all-start.2 = ((bf16[128,128,128]{2,1,0:T(8,128)(2,1)}), bf16[128,128,128]{2,1,0:T(8,128)(2,1)}, u32[]{:S(2)}, u32[]{:S(2)}) async-start(bf16[128,128,128]{2,1,0:T(8,128)(2,1)} %param.7), calls=%async_computation.2 | async-start | bytes 8388608 | tf_op jit(solution)/shard_map/all_to_all | solution.py:70
  51.4 3.1 %copy-start.3 = (bf16[4,1,64,576]{3,2,1,0:T(8,128)(2,1)S(1)}, bf16[4,1,64,576]{3,2,1,0:T(8,128)(2,1)}, u32[]{:S(2)}) copy-start(bf16[4,1,64,576]{3,2,1,0:T(8,128)(2,1)} %copy-done.2) | copy-start | bytes 884740
  61.9 2.3 %copy-start.4 = (bf16[4,64,576]{2,1,0:T(8,128)(2,1)S(1)}, bf16[4,64,576]{2,1,0:T(8,128)(2,1)}, u32[]{:S(2)}) copy-start(bf16[4,64,576]{2,1,0:T(8,128)(2,1)} %gather_fusion.1) | copy-start | bytes 884740
  64.2 1.0 copy-start.5
